TPU v7x, 256 devices: a whole 4x4x8 slice. The times are simulated.
256 devices in a mesh: cuts: 4 (over z_lo), amp: 64 (over y, x, z_hi, core).
Axes of the slice: x: 4, y: 4, z: 8 (z_hi: 2, z_lo: 4; z = z_hi * 4 + z_lo), core: 2. Of those that a mesh axis runs over, the one named last changes fastest.
Arguments:
- stem_state: bfloat16 [8, 32, 64, 128, 256], P('cuts', None, 'amp'), may hold values from -6 to 6
- gates: bfloat16 [8, 4, 2, 128, 128], P('cuts'), may hold values from -0.375 to 0.375
Outputs:
- amplitudes: float32 [32, 64, 128, 256], P('cuts', 'amp')
All inputs are finite; a program needn't handle non-finite values.
Results may differ from a plain program's by a relative error of at most 0.0049.
Values may be sent and summed in bfloat16 or wider, within the bound.
No kernel may reach another device: no remote copies, remote signals or barrier semaphores. Data moves between devices by JAX's collectives and lax.ppermute only.
A program may use at most 64 MiB of HBM per device.

v0:
```python
import jax
import jax.numpy as jnp
from jax import lax
from jax.sharding import PartitionSpec as P


def block_matrix(gate):
    real_part = gate[0]
    imag_part = gate[1]
    top = jnp.concatenate([real_part.T, imag_part.T], axis=1)
    bottom = jnp.concatenate([-imag_part.T, real_part.T], axis=1)
    return jnp.concatenate([top, bottom], axis=0)


def on_rows(values, real_gates, imag_gates):
    width = values.shape[-1] // 2
    first_term = jnp.einsum(
        "ska,shgac->shgkc", real_gates, values, preferred_element_type=jnp.float32
    )
    second_term = jnp.einsum(
        "ska,shgac->shgkc", imag_gates, values, preferred_element_type=jnp.float32
    )
    real_out = first_term[..., :width] - second_term[..., width:]
    imag_out = first_term[..., width:] + second_term[..., :width]
    return jnp.concatenate([real_out, imag_out], axis=-1)


def on_last(values, matrices):
    return jnp.einsum("shgac,scd->shgad", values, matrices, preferred_element_type=jnp.float32)


def per_device(stem_state, gates):
    groups = lax.axis_size("amp")
    slice_count, hidden, single, width, columns = stem_state.shape
    low = width // groups
    first = on_rows(stem_state, gates[:, 0, 0], gates[:, 0, 1]).astype(jnp.bfloat16)
    second_matrix = jax.vmap(block_matrix)(gates[:, 1])
    second = on_last(first, second_matrix).astype(jnp.bfloat16)
    split_state = second.reshape(slice_count, hidden, 1, groups, low, columns)
    last_matrix = jax.vmap(block_matrix)(gates[:, 3])
    pieces = lax.all_to_all(split_state, "amp", split_axis=3, concat_axis=2, tiled=True)
    count = pieces.shape[1]
    merged = pieces.reshape(slice_count, count, 1, width, columns)
    third = on_rows(merged, gates[:, 2, 0], gates[:, 2, 1]).astype(jnp.bfloat16)
    fourth = on_last(third, last_matrix).reshape(slice_count, count, width, columns)
    total = jnp.sum(fourth, axis=0)
    outgoing = total.reshape(hidden, groups, 1, low, columns)
    owned = lax.all_to_all(outgoing, "amp", split_axis=1, concat_axis=2, tiled=True)
    owned = owned.reshape(hidden, 1, width, columns)
    return lax.psum_scatter(owned, "cuts", scatter_dimension=0, tiled=True)


def solution(mesh):
    placed = (P("cuts", None, "amp", None, None), P("cuts", None, None, None, None))
    return jax.shard_map(
        per_device,
        mesh=mesh,
        in_specs=placed,
        out_specs=P("cuts", "amp", None, None),
        check_vma=False,
    )
```

profile of v0, /device:TPU:1, one launch (start us, length us, event | category | flops | bytes accessed | tf_op | source)
XLA Modules:
  0.0 385.8 jit_solution(2300316748091745869)
XLA Ops:
  6.5 0.0 copy-start.1
  6.5 0.0 copy-start.2
  6.5 7.3 %fusion.19 = f32[2,32,1,128,256]{3,4,1,0,2:T(8,128)} fusion(bf16[2,32,1,128,256]{4,3,2,1,0:T(8,128)(2,1)} %param.2, bf16[2,4,2,128,128]{4,3,2,1,0:T(8,128)(2,1)} %param.3), kind=kOutput, calls=%fused_computation.21 | convolution fusion | flops 536870912 | bytes 12648448 | tf_op jit(solution)/shard_map/ska,shgac->shgkc/dot_general | solution.py:20
  13.9 0.0 copy-done.1
  13.9 0.0 copy-done.2
  13.9 5.0 %fusion.16 = f32[2,32,1,128,256]{3,4,1,0,2:T(8,128)} fusion(bf16[2,32,1,128,256]{4,3,2,1,0:T(8,128)(2,1)S(1)} %copy-done.1, bf16[2,4,2,128,128]{4,3,2,1,0:T(8,128)(2,1)S(1)} %copy-done.2), kind=kOutput, calls=%fused_computation.20 | convolution fusion | flops 536870912 | bytes 12648448 | tf_op jit(solution)/shard_map/ska,shgac->shgkc/dot_general | solution.py:17
  18.9 0.1 copy.71
  19.1 6.8 %fusion.28 = (bf16[2,32,128,128]{2,3,1,0:T(8,128)(2,1)S(1)}, bf16[2,32,128,128]{2,3,1,0:T(8,128)(2,1)S(1)}) fusion(f32[2,32,1,128,256]{3,4,1,0,2:T(8,128)} %fusion.19, f32[2,32,1,128,256]{3,4,1,0,2:T(8,128)} %fusion.16), kind=kLoop, calls=%fused_computation.26 | loop fusion | flops 4194304 | bytes 20971520 | tf_op jit(solution)/shard_map/concatenate | solution.py:25
  25.9 3.3 fusion.22
  29.2 7.2 %reshape.67 = bf16[2,32,1,64,2,256]{5,4,3,1,0,2:T(2,128)(2,1)} reshape(bf16[2,32,128,256]{3,2,1,0:T(8,128)(2,1)} %fusion.22) | data formatting | bytes 8388608 | tf_op jit(solution)/shard_map/reshape | solution.py:39
  36.4 8.7 %copy.48 = bf16[2,32,1,64,2,256]{5,1,4,0,2,3:T(8,128)(2,1)} copy(bf16[2,32,1,64,2,256]{5,4,3,1,0,2:T(2,128)(2,1)} %reshape.67) | data formatting | bytes 8388608 | tf_op jit(solution)/shard_map/reshape | solution.py:39
  45.1 15.8 %all-to-all-start = ((bf16[2,32,1,64,2,256]{5,1,4,0,2,3:T(8,128)(2,1)}), bf16[2,32,1,64,2,256]{5,1,4,0,2,3:T(8,128)(2,1)}, u32[]{:S(2)}, u32[]{:S(2)}) async-start(bf16[2,32,1,64,2,256]{5,1,4,0,2,3:T(8,128)(2,1)} %copy.48), calls=%async_computation | async-start | bytes 8388608 | tf_op jit(solution)/shard_map/all_to_all | solution.py:41
  60.9 0.2 reduce-scatter.2.cloned.1.call-start
  61.2 0.1 copy.74
  61.3 100.2 %all-to-all-done = bf16[2,32,1,64,2,256]{5,1,4,0,2,3:T(8,128)(2,1)} async-done(((bf16[2,32,1,64,2,256]{5,1,4,0,2,3:T(8,128)(2,1)}), bf16[2,32,1,64,2,256]{5,1,4,0,2,3:T(8,128)(2,1)}, u32[]{:S(2)}, u32[]{:S(2)}) %all-to-all-start) | async-done | bytes 4194336 | tf_op jit(solution)/shard_map/all_to_all | solution.py:41
  161.6 5.0 %copy.49 = bf16[2,32,1,64,2,256]{5,1,4,3,0,2:T(8,128)(2,1)} copy(bf16[2,32,1,64,2,256]{5,1,4,0,2,3:T(8,128)(2,1)} %all-to-all-done) | data formatting | bytes 8388608 | tf_op jit(solution)/shard_map/all_to_all | solution.py:41
  166.6 7.9 %copy.51 = bf16[2,32,128,256]{2,3,1,0:T(8,128)(2,1)} copy(bf16[2,32,128,256]{3,1,2,0:T(8,128)(2,1)} %bitcast.110) | data formatting | bytes 8388608 | tf_op jit(solution)/shard_map/reshape.14
  174.4 0.0 copy-start
  174.4 3.6 convolution_bitcast_fusion
  178.0 0.0 copy-done
  178.0 1.2 convolution_bitcast_fusion.1
  179.3 1.8 fusion.30
  181.1 3.3 fusion.25
  184.4 5.9 %reshape.69 = f32[32,64,1,2,256]{4,3,1,0,2:T(2,128)} reshape(f32[32,128,256]{2,1,0:T(8,128)} %fusion.25) | data formatting | bytes 8388608 | tf_op jit(solution)/shard_map/reshape | solution.py:47
  190.2 4.6 %copy.56 = f32[32,64,1,2,256]{4,3,0,2,1:T(2,128)S(1)} copy(f32[32,64,1,2,256]{4,3,1,0,2:T(2,128)} %reshape.69) | data formatting | bytes 8388608 | tf_op jit(solution)/shard_map/reshape | solution.py:47
  194.8 59.1 %all_to_all.8 = f32[32,64,1,2,256]{4,3,0,2,1:T(2,128)S(1)} all-to-all(f32[32,64,1,2,256]{4,3,0,2,1:T(2,128)S(1)} %copy.56), channel_id=1, replica_groups=mesh['cuts'=4,'amp'=64] {'amp'}, dimensions={1} | all-to-all | bytes 8388608 | tf_op jit(solution)/shard_map/all_to_all | solution.py:48
  253.9 2.6 copy.57
  256.5 0.0 reduce-scatter.2.cloned.1.call-update
  256.5 119.9 %reduce-scatter.2.cloned.1.call-done = f32[8,1,128,256]{3,0,2,1:T(8,128)} async-done(((f32[32,1,128,256]{3,0,2,1:T(8,128)}), f32[8,1,128,256]{3,0,2,1:T(8,128)}) %reduce-scatter.2.cloned.1.call-update) | async-done | bytes 1048592 | tf_op jit(solution)/shard_map/reduce_scatter | solution.py:50
  376.4 2.5 copy.58
  (5 shorter events, 0.1 us)
Async XLA Ops:
  6.5 7.3 %copy-start.1 = (bf16[2,32,1,128,256]{4,3,2,1,0:T(8,128)(2,1)S(1)}, bf16[2,32,1,128,256]{4,3,2,1,0:T(8,128)(2,1)}, u32[]{:S(2)}) copy-start(bf16[2,32,1,128,256]{4,3,2,1,0:T(8,128)(2,1)} %param.2) | copy-start | bytes 12582916
  6.5 7.3 %copy-start.2 = (bf16[2,4,2,128,128]{4,3,2,1,0:T(8,128)(2,1)S(1)}, bf16[2,4,2,128,128]{4,3,2,1,0:T(8,128)(2,1)}, u32[]{:S(2)}) copy-start(bf16[2,4,2,128,128]{4,3,2,1,0:T(8,128)(2,1)} %param.3) | copy-start | bytes 1572868
  45.1 116.4 %all-to-all-start = ((bf16[2,32,1,64,2,256]{5,1,4,0,2,3:T(8,128)(2,1)}), bf16[2,32,1,64,2,256]{5,1,4,0,2,3:T(8,128)(2,1)}, u32[]{:S(2)}, u32[]{:S(2)}) async-start(bf16[2,32,1,64,2,256]{5,1,4,0,2,3:T(8,128)(2,1)} %copy.48), calls=%async_computation | async-start | bytes 8388608 | tf_op jit(solution)/shard_map/all_to_all | solution.py:41
  60.9 315.4 %reduce-scatter.2.cloned.1.call-start = ((), (), s32[]{:S(2)}) async-start(), calls=%async_computation.3 | async-start | bytes 5242880 | tf_op jit(solution)/shard_map/reduce_scatter | solution.py:50
  174.4 3.6 copy-start
Sparse Core Ops, SparseCore 0:
  256.6 119.7 reduce-scatter.1
where the time goes:
time: 386 us
  waiting for transfers between devices  220 us (57%)
  blocking collectives  59.1 us (15%)
  local copies, waits for them, and re-layouts  44.6 us (12%)
  matrix products  23.7 us (6%)
  starting transfers between devices  16 us (4%)
  between operations  13.5 us (3%)
  other arithmetic  8.67 us (2%)
    reduce_scatter x1, waiting for transfers between devices, per_device(): return lax.psum_scatter(owned, 'cuts', scatter_dimension=0, tiled=True)  120 us
    all_to_all x1, waiting for transfers between devices, per_device(): lax.all_to_all(split_state, 'amp', split_axis=3, concat_axis=2, tiled=True)  100 us
    all_to_all x1, blocking collectives, per_device(): lax.all_to_all(outgoing, 'amp', split_axis=1, concat_axis=2, tiled=True)  59.1 us
    reshape x2, local copies, waits for them, and re-layouts, per_device(): split_state = second.reshape(slice_count, hidden, 1, groups, low, columns)  15.9 us
    all_to_all x1, starting transfers between devices, per_device(): lax.all_to_all(split_state, 'amp', split_axis=3, concat_axis=2, tiled=True)  15.8 us
    dot_general x2, matrix products, on_rows(): jnp.einsum('ska,shgac->shgkc', imag_gates, values, preferred_element_type...  10.9 us
    reshape x2, local copies, waits for them, and re-layouts, per_device(): outgoing = total.reshape(hidden, groups, 1, low, columns)  10.4 us
    concatenate x2, other arithmetic, on_rows(): return jnp.concatenate([real_out, imag_out], axis=-1)  8.65 us
  transfers between devices with their start and end apart: 2, of which 2 were waited for; matrix products, arithmetic and copies ran while one was open for 0% of the time, Pallas kernels for 0%

commit v1 on v0

v1 whole, which is shorter than its diff:
```python
import jax
import jax.numpy as jnp
from jax import lax
from jax.experimental import pallas as pl
from jax.experimental.pallas import tpu as pltpu
from jax.sharding import Mesh, PartitionSpec as P

CHUNKS = 1
PLANE = ("y", "x", "core")
COLUMN = ("zh", "cuts")
BF = jnp.bfloat16
F32 = jnp.float32


def dot(left, right):
    return jnp.dot(left, right, preferred_element_type=F32)


def dot_t(left, right):
    return lax.dot_general(left, right, (((1,), (1,)), ((), ())), preferred_element_type=F32)


def iota(shape, axis):
    return lax.broadcasted_iota(jnp.int32, shape, axis)


def select_matrix(hit):
    return jnp.where(hit, 1.0, 0.0).astype(BF)


def prepare(zh_ref, gates_ref, rows_ref, second_ref, fourth_ref, joint_ref):
    zh = zh_ref[0]
    row, col = iota((256, 128), 0), iota((256, 128), 1)
    pick = select_matrix(((row >> 3) * 4 + (row & 3)) == col)
    row_h = (row >> 2) & 1
    row, col = iota((512, 128), 0), iota((512, 128), 1)
    d, q = (row >> 3) & 31, (row >> 2) & 1
    pick_out = select_matrix((((d >> 1) * 4 + (row >> 8) * 2 + (d & 1)) * 2 + q) == col)
    row, col = iota((128, 512), 0), iota((128, 512), 1)
    d, q = col >> 4, col & 1
    pick_in = select_matrix((((d >> 1) * 4 + zh * 2 + (d & 1)) * 2 + q) == row)
    row, col = iota((512, 512), 0), iota((512, 512), 1)
    same = (row & 3) == ((col >> 1) & 3)
    col_s = (col >> 3) & 1
    for s in range(2):
        for part in range(2):
            spread = dot(pick, gates_ref[s, 0, part])
            for h2 in range(2):
                begin = part * 256 + h2 * 128
                rows_ref[s, :, begin : begin + 128] = jnp.where(row_h == h2, spread, 0.0).astype(BF)
        for layer, out in ((1, second_ref), (3, fourth_ref)):
            real, imag = gates_ref[s, layer, 0], gates_ref[s, layer, 1]
            out[s, :128, :128] = real
            out[s, :128, 128:] = -imag
            out[s, 128:, :128] = imag
            out[s, 128:, 128:] = real
    for part in range(2):
        wide = []
        for s in range(2):
            wide.append(dot(dot(pick_out, gates_ref[s, 2, part]).astype(BF), pick_in))
        mixed = jnp.where(col_s == 0, wide[0], wide[1])
        joint_ref[:, part * 512 : part * 512 + 512] = jnp.where(same, mixed, 0.0).astype(BF)


def times_i(values):
    return jnp.concatenate([-values[:, 128:], values[:, :128]], axis=1)


def before(state_ref, rows_ref, second_ref, fourth_ref, out_ref):
    pieces = []
    for s in range(2):
        state = state_ref[s, 0, 0].reshape(256, 256)
        first = dot(rows_ref[s, :, :256], state) + dot(rows_ref[s, :, 256:], times_i(state))
        second = dot_t(first.astype(BF), second_ref[s])
        pieces.append(dot_t(second.astype(BF), fourth_ref[s]).reshape(32, 8, 256))
    out_ref[:, 0] = jnp.concatenate(pieces, axis=1).astype(BF)


def after(state_ref, joint_ref, out_ref):
    state = state_ref[:, 0].reshape(512, 256)
    total = dot(joint_ref[:, :512], state) + dot(joint_ref[:, 512:], times_i(state))
    out_ref[:, 0, 0] = total.astype(BF).reshape(2, 256, 256)


def place(state_ref, out_ref):
    row, col = iota((256, 256), 0), iota((256, 256), 1)
    d, j, q, h2 = (row >> 2) & 31, (row >> 1) & 1, row & 1, row >> 7
    order = select_matrix((d * 8 + q * 4 + h2 * 2 + j) == col)
    state = state_ref[:, 0].astype(F32).reshape(256, 256).astype(BF)
    out_ref[0] = dot(order, state).reshape(2, 128, 256)


def shape_of(shape, kind=BF):
    return jax.ShapeDtypeStruct(shape, kind)


def whole(shape):
    return pl.BlockSpec(shape, lambda *at: (0,) * len(shape))


def per_device(stem_state, gates):
    chunks = CHUNKS
    pairs = 4 // chunks
    zh = lax.axis_index("zh").astype(jnp.int32).reshape(1)
    rows, second, fourth, joint = pl.pallas_call(
        prepare,
        in_specs=[pl.BlockSpec(memory_space=pltpu.SMEM), pl.BlockSpec(memory_space=pltpu.VMEM)],
        out_shape=[shape_of((2, 256, 512)), shape_of((2, 256, 256)), shape_of((2, 256, 256)), shape_of((512, 1024))],
        name="prepare",
    )(zh, gates)
    state = stem_state.reshape(2, 4, 4, 2, 128, 256)
    sums = []
    for chunk in range(chunks):
        sent = pl.pallas_call(
            before,
            grid=(pairs, 4),
            in_specs=[
                pl.BlockSpec((2, 1, 1, 2, 128, 256), lambda hp, k, c=chunk: (0, k, c * pairs + hp, 0, 0, 0)),
                whole((2, 256, 512)),
                whole((2, 256, 256)),
                whole((2, 256, 256)),
            ],
            out_specs=pl.BlockSpec((32, 1, 16, 256), lambda hp, k: (0, hp * 4 + k, 0, 0)),
            out_shape=shape_of((32, pairs * 4, 16, 256)),
            name="before",
        )(state, rows, second, fourth)
        got = lax.all_to_all(sent, PLANE, split_axis=0, concat_axis=0, tiled=True)
        partial = pl.pallas_call(
            after,
            grid=(pairs, 4),
            in_specs=[
                pl.BlockSpec((32, 1, 16, 256), lambda hp, k: (0, hp * 4 + k, 0, 0)),
                whole((512, 1024)),
            ],
            out_specs=pl.BlockSpec((2, 1, 1, 256, 256), lambda hp, k: (0, k, hp, 0, 0)),
            out_shape=shape_of((2, 4, pairs, 256, 256)),
            name="after",
        )(got, joint)
        total = lax.psum_scatter(
            partial.reshape(8, pairs * 256, 256), COLUMN, scatter_dimension=0, tiled=True
        )
        sums.append(total.reshape(pairs, 32, 8, 256))
    home = jnp.swapaxes(jnp.concatenate(sums, axis=0), 0, 1)
    home = lax.all_to_all(home, PLANE, split_axis=0, concat_axis=0, tiled=True)
    placed = pl.pallas_call(
        place,
        grid=(4,),
        in_specs=[pl.BlockSpec((32, 1, 8, 256), lambda hp: (0, hp, 0, 0))],
        out_specs=pl.BlockSpec((1, 2, 128, 256), lambda hp: (hp, 0, 0, 0)),
        out_shape=shape_of((4, 2, 128, 256), F32),
        name="place",
    )(home)
    return placed.reshape(8, 1, 128, 256)


def solution(mesh):
    fine = Mesh(mesh.devices.reshape(4, 4, 4, 2, 2), ("cuts", "y", "x", "zh", "core"))
    amp = ("y", "x", "zh", "core")
    return jax.shard_map(
        per_device,
        mesh=fine,
        in_specs=(P("cuts", None, amp, None, None), P("cuts", None, None, None, None)),
        out_specs=P("cuts", amp, None, None),
        check_vma=False,
    )
```

time: 386 us -> 185 us (0.48)
  waiting for transfers between devices: 220 us -> 54.5 us
  local copies, waits for them, and re-layouts: 44.6 us -> 1.09 us
  Pallas kernels: 0 us -> 37 us
  matrix products: 23.7 us -> 0 us
  blocking collectives: 59.1 us -> 78.4 us
  starting transfers between devices: 16 us -> 0.01 us
  other arithmetic: 8.67 us -> 0 us
    all_to_all x1 -> x0, waiting for transfers between devices: 100 us -> none  [per_device(): lax.all_to_all(split_state, 'amp', split_axis=3, concat_axis=2, tiled=True)]
    reduce_scatter x1, waiting for transfers between devices: 120 us -> 54.5 us  [per_device(): lax.psum_scatter(partial.reshape(8, pairs * 256, 256), COLUMN, scatter_di...]
    pallas_call x0 -> x4, Pallas kernels: none -> 37 us  [the longest x1 16.1 us: per_device(): pl.pallas_call(before, grid=(pairs, 4), in_specs=[pl.BlockSpec((2, 1, 1,...]
    reshape x4 -> x1, local copies, waits for them, and re-layouts: 26.3 us -> 1.09 us  [per_device(): sums.append(total.reshape(pairs, 32, 8, 256))]
    dot_general x6 -> x0, matrix products: 23.7 us -> none  [the longest x2 10.9 us: on_rows(): jnp.einsum('ska,shgac->shgkc', imag_gates, values, preferred_element_type...]
    all_to_all x1 -> x2, blocking collectives: 59.1 us -> 78.4 us  [the longest x1 59.4 us: per_device(): got = lax.all_to_all(sent, PLANE, split_axis=0, concat_axis=0, tiled=True)]
    all_to_all x1 -> x0, starting transfers between devices: 15.8 us -> none  [per_device(): lax.all_to_all(split_state, 'amp', split_axis=3, concat_axis=2, tiled=True)]
    concatenate x2 -> x0, other arithmetic: 8.65 us -> none  [on_rows(): return jnp.concatenate([real_out, imag_out], axis=-1)]
  transfers between devices with their start and end apart: 2 -> 1, of which waited for: 2 -> 1; matrix products, arithmetic and copies ran while one was open for 0% -> 0% of each run, Pallas kernels for 0% -> 0%
where the time goes in v1:
time: 185 us; the launch traced here: 184 us
  blocking collectives  78.4 us (42%)
  waiting for transfers between devices  54.5 us (29%)
  Pallas kernels  37 us (20%)
  between operations  13.4 us (7%)
    all_to_all x1, blocking collectives, per_device(): got = lax.all_to_all(sent, PLANE, split_axis=0, concat_axis=0, tiled=True)  59.4 us
    reduce_scatter x1, waiting for transfers between devices, per_device(): lax.psum_scatter(partial.reshape(8, pairs * 256, 256), COLUMN, scatter_di...  54.5 us
    all_to_all x1, blocking collectives, per_device(): home = lax.all_to_all(home, PLANE, split_axis=0, concat_axis=0, tiled=True)  18.9 us
    pallas_call x1, Pallas kernels, per_device(): pl.pallas_call(before, grid=(pairs, 4), in_specs=[pl.BlockSpec((2, 1, 1,...  16.1 us
    pallas_call x1, Pallas kernels, per_device(): pl.pallas_call(after, grid=(pairs, 4), in_specs=[pl.BlockSpec((32, 1, 16,...  13.7 us
  transfers between devices with their start and end apart: 1, of which 1 were waited for; matrix products, arithmetic and copies ran while one was open for 0% of the time, Pallas kernels for 0%

profile of v1, /device:TPU:1, one launch (start us, length us, event | category | flops | bytes accessed | tf_op | source)
XLA Modules:
  0.0 184.3 jit_solution(17913376380627454619)
XLA Ops:
  6.5 0.0 reduce-scatter.2.cloned.1.call-start
  6.5 3.5 %prepare.1 = (bf16[2,256,512]{2,1,0:T(8,128)(2,1)}, bf16[2,256,256]{2,1,0:T(8,128)(2,1)}, bf16[2,256,256]{2,1,0:T(8,128)(2,1)}, bf16[512,1024]{1,0:T(8,128)(2,1)}) custom-call(s32[1]{0:T(128)} %bitcast.1.zh_ref, bf16[2,4,2,128,128]{4,3,2,1,0:T(8,128)(2,1)} %gates_ref.1), custom_call_target="tpu_custom_call" | custom-call | tf_op jit(solution)/shard_map/prepare/pallas_call | solution.py:105
  10.1 16.1 %before.1 = bf16[32,16,16,256]{3,2,1,0:T(8,128)(2,1)} custom-call(bf16[2,4,4,2,128,256]{5,4,3,2,1,0:T(8,128)(2,1)} %bitcast.11, bf16[2,256,512]{2,1,0:T(8,128)(2,1)} %get-tuple-element.9.rows_ref, bf16[2,256,256]{2,1,0:T(8,128)(2,1)} %get-tuple-element.10.second_ref, bf16[2,256,256]{2,1,0:T(8,128)(2,1)} %get-tuple-element.11.fourth_ref), custom_call_target="tpu_custom_call" | custom-call | tf_op jit(solution)/shard_map/before/pallas_call | solution.py:114
  26.1 59.4 %all_to_all.10.state_ref = bf16[32,16,16,256]{3,2,1,0:T(8,128)(2,1)} all-to-all(bf16[32,16,16,256]{3,2,1,0:T(8,128)(2,1)} %before.1), channel_id=1, replica_groups=mesh['cuts'=4,'y'=4,'x'=4,'zh'=2,'core'=2] {'y','x','core'}, dimensions={0} | all-to-all | bytes 8388608 | tf_op jit(solution)/shard_map/all_to_all | solution.py:127
  85.6 13.7 %after.1 = bf16[2,4,4,256,256]{4,3,2,1,0:T(8,128)(2,1)} custom-call(bf16[32,16,16,256]{3,2,1,0:T(8,128)(2,1)} %all_to_all.10.state_ref, bf16[512,1024]{1,0:T(8,128)(2,1)} %get-tuple-element.12.joint_ref), custom_call_target="tpu_custom_call" | custom-call | tf_op jit(solution)/shard_map/after/pallas_call | solution.py:128
  99.3 0.0 reduce-scatter.2.cloned.1.call-update
  99.3 54.5 %reduce-scatter.2.cloned.1.call-done = bf16[1,1024,256]{2,1,0:T(8,128)(2,1)} async-done(((bf16[8,1024,256]{2,1,0:T(8,128)(2,1)}), bf16[1,1024,256]{2,1,0:T(8,128)(2,1)}) %reduce-scatter.2.cloned.1.call-update) | async-done | bytes 524304 | tf_op jit(solution)/shard_map/reduce_scatter | solution.py:139
  153.8 1.1 copy.7
  154.9 18.9 %all_to_all.11.state_ref = bf16[32,4,8,256]{3,2,1,0:T(8,128)(2,1)} all-to-all(bf16[32,4,8,256]{3,2,1,0:T(8,128)(2,1)S(1)} %bitcast.12), channel_id=1, replica_groups=mesh['cuts'=4,'y'=4,'x'=4,'zh'=2,'core'=2] {'y','x','core'}, dimensions={0} | all-to-all | bytes 1048576 | tf_op jit(solution)/shard_map/all_to_all | solution.py:144
  173.9 3.6 %place.1 = f32[4,2,128,256]{3,2,1,0:T(8,128)} custom-call(bf16[32,4,8,256]{3,2,1,0:T(8,128)(2,1)} %all_to_all.11.state_ref), custom_call_target="tpu_custom_call" | custom-call | tf_op jit(solution)/shard_map/place/pallas_call | solution.py:145
Async XLA Ops:
  6.5 147.3 %reduce-scatter.2.cloned.1.call-start = ((), (), s32[]{:S(2)}) async-start(), calls=%async_computation.3 | async-start | bytes 4718592 | tf_op jit(solution)/shard_map/reduce_scatter | solution.py:139
Sparse Core Ops, SparseCore 0:
  99.5 54.3 reduce-scatter.1

commit v2 on v1

v2 whole, which is shorter than its diff:
```python
import functools

import jax
import jax.numpy as jnp
from jax import lax
from jax.experimental import pallas as pl
from jax.experimental.pallas import tpu as pltpu
from jax.sharding import Mesh, PartitionSpec as P


CHUNKS = 2
PLANE = ("y", "x", "core")
COLUMN = ("cuts", "zh")
BF = jnp.bfloat16
F32 = jnp.float32


def dot(left, right):
    return jnp.dot(left, right, preferred_element_type=F32)


def dot_t(left, right):
    return lax.dot_general(left, right, (((1,), (1,)), ((), ())), preferred_element_type=F32)


def iota(shape, axis):
    return lax.broadcasted_iota(jnp.int32, shape, axis)


def select_matrix(hit):
    return jnp.where(hit, 1.0, 0.0).astype(BF)


def before(gates_ref, state_ref, out_ref, rows_ref, second_ref, fourth_ref):
    @pl.when(pl.program_id(0) == 0)
    def prepare():
        row, col = iota((256, 128), 0), iota((256, 128), 1)
        pick = select_matrix(((row >> 3) * 4 + (row & 3)) == col)
        row_h = (row >> 2) & 1
        for s in range(2):
            for part in range(2):
                spread = dot(pick, gates_ref[s, 0, part])
                for h2 in range(2):
                    begin = part * 256 + h2 * 128
                    rows_ref[s, :, begin : begin + 128] = jnp.where(row_h == h2, spread, 0.0).astype(BF)
            for layer, out in ((1, second_ref), (3, fourth_ref)):
                real, imag = gates_ref[s, layer, 0], gates_ref[s, layer, 1]
                out[s, :128, :128] = real
                out[s, :128, 128:] = -imag
                out[s, 128:, :128] = imag
                out[s, 128:, 128:] = real

    results = []
    for s in range(2):
        firsts = []
        for k in range(4):
            state = state_ref[s, k, 0].reshape(256, 256)
            first = dot(rows_ref[s, :, :256], state) + dot(rows_ref[s, :, 256:], times_i(state))
            firsts.append(first.astype(BF))
        second = dot_t(jnp.concatenate(firsts, axis=0), second_ref[s]).astype(BF)
        results.append(dot_t(second, fourth_ref[s]).reshape(4, 32, 8, 256))
    for k in range(4):
        out_ref[:, k] = jnp.concatenate([results[0][k], results[1][k]], axis=1).astype(BF)


def join(z_ref, gates_ref, joint_ref):
    zh = z_ref[0] >> 2
    row, col = iota((512, 128), 0), iota((512, 128), 1)
    d, q = (row >> 3) & 31, (row >> 2) & 1
    pick_out = select_matrix((((d >> 1) * 4 + (row >> 8) * 2 + (d & 1)) * 2 + q) == col)
    row, col = iota((128, 512), 0), iota((128, 512), 1)
    d, q = col >> 4, col & 1
    pick_in = select_matrix((((d >> 1) * 4 + zh * 2 + (d & 1)) * 2 + q) == row)
    row, col = iota((512, 512), 0), iota((512, 512), 1)
    same = (row & 3) == ((col >> 1) & 3)
    col_s = (col >> 3) & 1
    for part in range(2):
        wide = []
        for s in range(2):
            wide.append(dot(dot(pick_out, gates_ref[s, 2, part]).astype(BF), pick_in))
        mixed = jnp.where(col_s == 0, wide[0], wide[1])
        joint_ref[:, part * 512 : part * 512 + 512] = jnp.where(same, mixed, 0.0).astype(BF)


def times_i(values):
    return jnp.concatenate([-values[:, 128:], values[:, :128]], axis=1)


def after(way, z_ref, state_ref, joint_ref, *out_refs):
    z = z_ref[0]
    states = [state_ref[:, (z + way * step) & 3].reshape(512, 256) for step in range(4)]
    turned = [times_i(state) for state in states]
    total = dot(joint_ref[:, :512], jnp.concatenate(states, axis=1))
    total = total + dot(joint_ref[:, 512:], jnp.concatenate(turned, axis=1))
    total = total.astype(BF)
    for step in range(4):
        low, high = (total[half * 256 : half * 256 + 256, step * 256 : step * 256 + 256] for half in range(2))
        ahead = (((z + way * step) & 3) - z) & 7
        ahead = jnp.full((256, 256), ahead, jnp.int32)
        place = (way * step) & 3
        out_refs[place][0] = jnp.where(ahead < 4, low, high)
        out_refs[place + 4][0] = jnp.where(ahead < 4, high, low)


def place(state_ref, out_ref):
    row, col = iota((256, 256), 0), iota((256, 256), 1)
    d, j, q, h2 = (row >> 2) & 31, (row >> 1) & 1, row & 1, row >> 7
    order = select_matrix((d * 8 + q * 4 + h2 * 2 + j) == col)
    state = state_ref[:, 0].astype(F32).reshape(256, 256).astype(BF)
    out_ref[0] = dot(order, state).reshape(2, 128, 256)


def ring(step):
    def at(z):
        return (z % 4) * 2 + z // 4

    return [(at(z), at((z + step) % 8)) for z in range(8)]


def add(*values):
    total = values[0].astype(F32)
    for value in values[1:]:
        total = total + value.astype(F32)
    return total.astype(BF)


def reduce_column(blocks, way):
    near, far = blocks[4], blocks[-3 * way & 7]
    for step in range(1, 5):
        near = lax.ppermute(near, COLUMN, ring(way))
        if step < 4:
            near = add(near, blocks[(4 - step) * way & 7])
            far = lax.ppermute(far, COLUMN, ring(-way))
        if step < 3:
            far = add(far, blocks[(step - 3) * way & 7])
    return add(near, far, blocks[0])


def shape_of(shape, kind=BF):
    return jax.ShapeDtypeStruct(shape, kind)


def whole(shape):
    return pl.BlockSpec(shape, lambda *at: (0,) * len(shape))


def per_device_steps(stem_state, gates):
    chunks = CHUNKS
    pairs = 4 // chunks
    z = (lax.axis_index("zh") * 4 + lax.axis_index("cuts")).astype(jnp.int32).reshape(1)
    scalar = pl.BlockSpec(memory_space=pltpu.SMEM)
    joint = pl.pallas_call(
        join,
        in_specs=[scalar, pl.BlockSpec(memory_space=pltpu.VMEM)],
        out_shape=shape_of((512, 1024)),
        name="join",
    )(z, gates)
    state = stem_state.reshape(2, 4, 4, 2, 128, 256)
    sums = []
    for chunk in range(chunks):
        way = 1 - 2 * (chunk & 1)
        sent = pl.pallas_call(
            before,
            grid=(pairs,),
            in_specs=[
                whole((2, 4, 2, 128, 128)),
                pl.BlockSpec((2, 4, 1, 2, 128, 256), lambda hp, c=chunk: (0, 0, c * pairs + hp, 0, 0, 0)),
            ],
            out_specs=pl.BlockSpec((32, 4, 16, 256), lambda hp: (0, hp, 0, 0)),
            out_shape=shape_of((32, pairs * 4, 16, 256)),
            scratch_shapes=[
                pltpu.VMEM((2, 256, 512), BF),
                pltpu.VMEM((2, 256, 256), BF),
                pltpu.VMEM((2, 256, 256), BF),
            ],
            name="before",
        )(gates, state)
        got = lax.all_to_all(sent, PLANE, split_axis=0, concat_axis=0, tiled=True)
        blocks = pl.pallas_call(
            functools.partial(after, way),
            grid=(pairs,),
            in_specs=[
                scalar,
                pl.BlockSpec((32, 4, 16, 256), lambda hp: (0, hp, 0, 0)),
                whole((512, 1024)),
            ],
            out_specs=[pl.BlockSpec((1, 256, 256), lambda hp: (hp, 0, 0))] * 8,
            out_shape=[shape_of((pairs, 256, 256))] * 8,
        )(z, got, joint)
        total = reduce_column(blocks, way)
        sums.append(total.reshape(pairs, 32, 8, 256))
    home = jnp.swapaxes(jnp.concatenate(sums, axis=0), 0, 1)
    home = lax.all_to_all(home, PLANE, split_axis=0, concat_axis=0, tiled=True)
    placed = pl.pallas_call(
        place,
        grid=(4,),
        in_specs=[pl.BlockSpec((32, 1, 8, 256), lambda hp: (0, hp, 0, 0))],
        out_specs=pl.BlockSpec((1, 2, 128, 256), lambda hp: (hp, 0, 0, 0)),
        out_shape=shape_of((4, 2, 128, 256), F32),
        name="place",
    )(home)
    return placed.reshape(8, 1, 128, 256)


def solution(mesh):
    fine = Mesh(mesh.devices.reshape(4, 4, 4, 2, 2), ("cuts", "y", "x", "zh", "core"))
    amp = ("y", "x", "zh", "core")
    return jax.shard_map(
        per_device_steps,
        mesh=fine,
        in_specs=(P("cuts", None, amp, None, None), P("cuts", None, None, None, None)),
        out_specs=P("cuts", amp, None, None),
        check_vma=False,
    )
```

time: 185 us -> 150 us (0.81)
  blocking collectives: 78.4 us -> 23.7 us
  starting transfers between devices: 0.01 us -> 38.7 us
  between operations: 13.4 us -> 0.22 us
  Pallas kernels: 37 us -> 27.9 us
  other arithmetic: 0 us -> 1.87 us
    all_to_all x2 -> x1, blocking collectives: 78.4 us -> 23.7 us  [per_device_steps(): home = lax.all_to_all(home, PLANE, split_axis=0, concat_axis=0, tiled=True)]
    reduce_scatter x1 -> x0, waiting for transfers between devices: 54.5 us -> none  [per_device(): lax.psum_scatter(partial.reshape(8, pairs * 256, 256), COLUMN, scatter_di...]
    all_to_all x0 -> x2, waiting for transfers between devices: none -> 37.4 us  [per_device_steps(): got = lax.all_to_all(sent, PLANE, split_axis=0, concat_axis=0, tiled=True)]
    ppermute x0 -> x14, starting transfers between devices: none -> 24.8 us  [the longest x8 17.5 us: reduce_column(): near = lax.ppermute(near, COLUMN, ring(way))]
    ppermute x0 -> x14, waiting for transfers between devices: none -> 17.4 us  [the longest x8 12.3 us: reduce_column(): near = lax.ppermute(near, COLUMN, ring(way))]
    all_to_all x0 -> x2, starting transfers between devices: none -> 14 us  [per_device_steps(): got = lax.all_to_all(sent, PLANE, split_axis=0, concat_axis=0, tiled=True)]
    pallas_call x4 -> x6, Pallas kernels: 37 us -> 27.9 us  [the longest x2 10.9 us: per_device_steps(): pl.pallas_call(before, grid=(pairs,), in_specs=[whole((2, 4, 2, 128, 128)...]
    unnamed x0 -> x26, local copies, waits for them, and re-layouts: none -> 2.73 us
  transfers between devices with their start and end apart: 1 -> 16, of which waited for: 1 -> 8; matrix products, arithmetic and copies ran while one was open for 0% -> 1% of each run, Pallas kernels for 0% -> 13%
where the time goes in v2:
time: 150 us
  waiting for transfers between devices  54.8 us (37%)
  starting transfers between devices  38.7 us (26%)
  Pallas kernels  27.9 us (19%)
  blocking collectives  23.7 us (16%)
  local copies, waits for them, and re-layouts  2.73 us (2%)
  other arithmetic  1.87 us (1%)
    all_to_all x2, waiting for transfers between devices, per_device_steps(): got = lax.all_to_all(sent, PLANE, split_axis=0, concat_axis=0, tiled=True)  37.4 us
    all_to_all x1, blocking collectives, per_device_steps(): home = lax.all_to_all(home, PLANE, split_axis=0, concat_axis=0, tiled=True)  23.7 us
    ppermute x8, starting transfers between devices, reduce_column(): near = lax.ppermute(near, COLUMN, ring(way))  17.5 us
    all_to_all x2, starting transfers between devices, per_device_steps(): got = lax.all_to_all(sent, PLANE, split_axis=0, concat_axis=0, tiled=True)  14 us
    ppermute x8, waiting for transfers between devices, reduce_column(): near = lax.ppermute(near, COLUMN, ring(way))  12.3 us
    pallas_call x2, Pallas kernels, per_device_steps(): pl.pallas_call(before, grid=(pairs,), in_specs=[whole((2, 4, 2, 128, 128)...  10.9 us
    pallas_call x2, Pallas kernels, per_device_steps(): pl.pallas_call(functools.partial(after, way), grid=(pairs,), in_specs=[sc...  10.1 us
    ppermute x6, starting transfers between devices, reduce_column(): far = lax.ppermute(far, COLUMN, ring(-way))  7.29 us
  transfers between devices with their start and end apart: 16, of which 8 were waited for; matrix products, arithmetic and copies ran while one was open for 1% of the time, Pallas kernels for 13%

profile of v2, /device:TPU:1, one launch (start us, length us, event | category | flops | bytes accessed | tf_op | source)
XLA Modules:
  0.0 149.9 jit_solution(2394631816114537158)
XLA Ops:
  0.0 5.5 %before.3 = bf16[32,8,16,256]{3,2,1,0:T(8,128)(2,1)} custom-call(bf16[2,4,2,128,128]{4,3,2,1,0:T(8,128)(2,1)} %gates_ref.5, bf16[2,4,4,2,128,256]{5,4,3,2,1,0:T(8,128)(2,1)} %bitcast.11), custom_call_target="tpu_custom_call" | custom-call | tf_op jit(solution)/shard_map/before/pallas_call | solution.py:162
  5.5 8.6 %all-to-all-start.1 = ((bf16[32,8,16,256]{3,2,1,0:T(8,128)(2,1)}), bf16[32,8,16,256]{3,2,1,0:T(8,128)(2,1)S(1)}, u32[]{:S(2)}, u32[]{:S(2)}) async-start(bf16[32,8,16,256]{3,2,1,0:T(8,128)(2,1)} %before.3), calls=%async_computation.1 | async-start | bytes 4194304 | tf_op jit(solution)/shard_map/all_to_all | solution.py:178
  14.1 5.5 %before.2 = bf16[32,8,16,256]{3,2,1,0:T(8,128)(2,1)} custom-call(bf16[2,4,2,128,128]{4,3,2,1,0:T(8,128)(2,1)} %gates_ref.5, bf16[2,4,4,2,128,256]{5,4,3,2,1,0:T(8,128)(2,1)} %bitcast.12), custom_call_target="tpu_custom_call" | custom-call | tf_op jit(solution)/shard_map/before/pallas_call | solution.py:162
  19.5 23.1 %all-to-all-done.1.state_ref = bf16[32,8,16,256]{3,2,1,0:T(8,128)(2,1)S(1)} async-done(((bf16[32,8,16,256]{3,2,1,0:T(8,128)(2,1)}), bf16[32,8,16,256]{3,2,1,0:T(8,128)(2,1)S(1)}, u32[]{:S(2)}, u32[]{:S(2)}) %all-to-all-start.1) | async-done | bytes 2097184 | tf_op jit(solution)/shard_map/all_to_all | solution.py:178
  42.6 1.3 copy-done.1
  44.0 5.4 %all-to-all-start = ((bf16[32,8,16,256]{3,2,1,0:T(8,128)(2,1)}), bf16[32,8,16,256]{3,2,1,0:T(8,128)(2,1)S(1)}, u32[]{:S(2)}, u32[]{:S(2)}) async-start(bf16[32,8,16,256]{3,2,1,0:T(8,128)(2,1)} %before.2), calls=%async_computation | async-start | bytes 4194304 | tf_op jit(solution)/shard_map/all_to_all | solution.py:178
  49.4 3.3 %join.1.joint_ref = bf16[512,1024]{1,0:T(8,128)(2,1)} custom-call(s32[1]{0:T(128)} %bitcast.z_ref, bf16[2,4,2,128,128]{4,3,2,1,0:T(8,128)(2,1)} %gates_ref.5), custom_call_target="tpu_custom_call" | custom-call | tf_op jit(solution)/shard_map/join/pallas_call | solution.py:152
  52.7 5.1 %shard_map.29 = (bf16[2,256,256]{2,1,0:T(8,128)(2,1)}, bf16[2,256,256]{2,1,0:T(8,128)(2,1)}, bf16[2,256,256]{2,1,0:T(8,128)(2,1)}, bf16[2,256,256]{2,1,0:T(8,128...) custom-call(s32[1]{0:T(128)} %bitcast.z_ref, ...), custom_call_target="tpu_custom_call" | custom-call | tf_op jit(solution)/shard_map/pallas_call | solution.py:179
  57.7 5.7 %collective-permute-start.7 = (bf16[2,256,256]{2,1,0:T(8,128)(2,1)}, bf16[2,256,256]{2,1,0:T(8,128)(2,1)S(1)}, u32[]{:S(2)}, u32[]{:S(2)}) collective-permute-start(bf16[2,256,256]{2,1,0:T(8,128)(2,1)} %get-tuple-element.29), channel_id=1, source_target_pairs={{0,194},{64,0},{128,64},{192,128},{2,192},{66,2},{130,66},{194,130... | collective-permute-start | bytes 786440 | tf_op jit(solution)/shard_map/ppermute | solution.py:130
  63.4 14.2 %all-to-all-done.state_ref = bf16[32,8,16,256]{3,2,1,0:T(8,128)(2,1)S(1)} async-done(((bf16[32,8,16,256]{3,2,1,0:T(8,128)(2,1)}), bf16[32,8,16,256]{3,2,1,0:T(8,128)(2,1)S(1)}, u32[]{:S(2)}, u32[]{:S(2)}) %all-to-all-start) | async-done | bytes 2097184 | tf_op jit(solution)/shard_map/all_to_all | solution.py:178
  77.7 1.4 copy-done
  79.0 5.0 %shard_map.28 = (bf16[2,256,256]{2,1,0:T(8,128)(2,1)}, bf16[2,256,256]{2,1,0:T(8,128)(2,1)}, bf16[2,256,256]{2,1,0:T(8,128)(2,1)}, bf16[2,256,256]{2,1,0:T(8,128...) custom-call(s32[1]{0:T(128)} %bitcast.z_ref, ...), custom_call_target="tpu_custom_call" | custom-call | tf_op jit(solution)/shard_map/pallas_call | solution.py:179
  84.1 1.7 %collective-permute-start = (bf16[2,256,256]{2,1,0:T(8,128)(2,1)}, bf16[2,256,256]{2,1,0:T(8,128)(2,1)S(1)}, u32[]{:S(2)}, u32[]{:S(2)}) collective-permute-start(bf16[2,256,256]{2,1,0:T(8,128)(2,1)} %get-tuple-element.21), channel_id=1, source_target_pairs={{0,64},{64,128},{128,192},{192,2},{2,66},{66,130},{130,194},{194,0... | collective-permute-start | bytes 786440 | tf_op jit(solution)/shard_map/ppermute | solution.py:130
  85.8 4.0 %collective-permute-start.4 = (bf16[2,256,256]{2,1,0:T(8,128)(2,1)}, bf16[2,256,256]{2,1,0:T(8,128)(2,1)S(1)}, u32[]{:S(2)}, u32[]{:S(2)}) collective-permute-start(bf16[2,256,256]{2,1,0:T(8,128)(2,1)} %get-tuple-element.25), channel_id=1, source_target_pairs={{0,194},{64,0},{128,64},{192,128},{2,192},{66,2},{130,66},{194,130... | collective-permute-start | bytes 786440 | tf_op jit(solution)/shard_map/ppermute | solution.py:133
  89.9 1.5 collective-permute-start.8
  91.4 0.3 collective-permute-start.12
  91.8 2.7 %collective-permute-done = bf16[2,256,256]{2,1,0:T(8,128)(2,1)S(1)} collective-permute-done((bf16[2,256,256]{2,1,0:T(8,128)(2,1)}, bf16[2,256,256]{2,1,0:T(8,128)(2,1)S(1)}, u32[]{:S(2)}, u32[]{:S(2)}) %collective-permute-start) | collective-permute-done | bytes 262176 | tf_op jit(solution)/shard_map/ppermute | solution.py:130
  94.5 1.0 add_convert_fusion.11
  95.7 2.7 %collective-permute-start.5 = (bf16[2,256,256]{2,1,0:T(8,128)(2,1)S(1)}, bf16[2,256,256]{2,1,0:T(8,128)(2,1)S(1)}, u32[]{:S(2)}, u32[]{:S(2)}) collective-permute-start(bf16[2,256,256]{2,1,0:T(8,128)(2,1)S(1)} %add_convert_fusion.8), channel_id=1, source_target_pairs={{0,194},{64,0},{128,64},{192,128},{2,192},{66,2},{130,66},{194,130... | collective-permute-start | bytes 786440 | tf_op jit(solution)/shard_map/ppermute | solution.py:133
  98.4 0.7 collective-permute-done.8
  99.3 3.5 %collective-permute-start.9 = (bf16[2,256,256]{2,1,0:T(8,128)(2,1)S(1)}, bf16[2,256,256]{2,1,0:T(8,128)(2,1)S(1)}, u32[]{:S(2)}, u32[]{:S(2)}) collective-permute-start(bf16[2,256,256]{2,1,0:T(8,128)(2,1)S(1)} %add_convert_fusion.4), channel_id=1, source_target_pairs={{0,194},{64,0},{128,64},{192,128},{2,192},{66,2},{130,66},{194,130... | collective-permute-start | bytes 786440 | tf_op jit(solution)/shard_map/ppermute | solution.py:130
  102.9 2.9 %collective-permute-done.1 = bf16[2,256,256]{2,1,0:T(8,128)(2,1)S(1)} collective-permute-done((bf16[2,256,256]{2,1,0:T(8,128)(2,1)S(1)}, bf16[2,256,256]{2,1,0:T(8,128)(2,1)S(1)}, u32[]{:S(2)}, u32[]{:S(2)}) %collective-permute-start.1) | collective-permute-done | bytes 262176 | tf_op jit(solution)/shard_map/ppermute | solution.py:130
  106.0 4.5 %collective-permute-done.9 = bf16[2,256,256]{2,1,0:T(8,128)(2,1)S(1)} collective-permute-done((bf16[2,256,256]{2,1,0:T(8,128)(2,1)S(1)}, bf16[2,256,256]{2,1,0:T(8,128)(2,1)S(1)}, u32[]{:S(2)}, u32[]{:S(2)}) %collective-permute-start.9) | collective-permute-done | bytes 262176 | tf_op jit(solution)/shard_map/ppermute | solution.py:130
  110.5 3.5 %collective-permute-start.10 = (bf16[2,256,256]{2,1,0:T(8,128)(2,1)S(1)}, bf16[2,256,256]{2,1,0:T(8,128)(2,1)S(1)}, u32[]{:S(2)}, u32[]{:S(2)}) collective-permute-start(bf16[2,256,256]{2,1,0:T(8,128)(2,1)S(1)} %add_convert_fusion.3), channel_id=1, source_target_pairs={{0,194},{64,0},{128,64},{192,128},{2,192},{66,2},{130,66},{194,130... | collective-permute-start | bytes 786440 | tf_op jit(solution)/shard_map/ppermute | solution.py:130
  114.0 0.1 collective-permute-start.6
  114.2 1.5 %collective-permute-start.3 = (bf16[2,256,256]{2,1,0:T(8,128)(2,1)S(1)}, bf16[2,256,256]{2,1,0:T(8,128)(2,1)S(1)}, u32[]{:S(2)}, u32[]{:S(2)}) collective-permute-start(bf16[2,256,256]{2,1,0:T(8,128)(2,1)S(1)} %add_convert_fusion.9), channel_id=1, source_target_pairs={{0,64},{64,128},{128,192},{192,2},{2,66},{66,130},{130,194},{194,0... | collective-permute-start | bytes 786440 | tf_op jit(solution)/shard_map/ppermute | solution.py:130
  115.8 1.5 %collective-permute-done.10 = bf16[2,256,256]{2,1,0:T(8,128)(2,1)S(1)} collective-permute-done((bf16[2,256,256]{2,1,0:T(8,128)(2,1)S(1)}, bf16[2,256,256]{2,1,0:T(8,128)(2,1)S(1)}, u32[]{:S(2)}, u32[]{:S(2)}) %collective-permute-start.10) | collective-permute-done | bytes 262176 | tf_op jit(solution)/shard_map/ppermute | solution.py:130
  117.3 0.1 fusion.1
  117.4 5.0 %collective-permute-done.6 = bf16[2,256,256]{2,1,0:T(8,128)(2,1)S(1)} collective-permute-done((bf16[2,256,256]{2,1,0:T(8,128)(2,1)S(1)}, bf16[2,256,256]{2,1,0:T(8,128)(2,1)S(1)}, u32[]{:S(2)}, u32[]{:S(2)}) %collective-permute-start.6) | collective-permute-done | bytes 262176 | tf_op jit(solution)/shard_map/ppermute | solution.py:133
  122.5 0.1 fusion
  122.6 23.7 %all_to_all.15.state_ref = bf16[32,4,8,256]{3,2,1,0:T(8,128)(2,1)} all-to-all(bf16[32,4,8,256]{3,2,1,0:T(8,128)(2,1)S(1)} %copy_bitcast_fusion), channel_id=1, replica_groups=mesh['cuts'=4,'y'=4,'x'=4,'zh'=2,'core'=2] {'y','x','core'}, dimensions={0} | all-to-all | bytes 1048576 | tf_op jit(solution)/shard_map/all_to_all | solution.py:193
  146.3 3.6 %place.1 = f32[4,2,128,256]{3,2,1,0:T(8,128)} custom-call(bf16[32,4,8,256]{3,2,1,0:T(8,128)(2,1)} %all_to_all.15.state_ref), custom_call_target="tpu_custom_call" | custom-call | tf_op jit(solution)/shard_map/place/pallas_call | solution.py:194
  (46 shorter events, 1.0 us)
Async XLA Ops:
  5.5 37.2 %all-to-all-start.1 = ((bf16[32,8,16,256]{3,2,1,0:T(8,128)(2,1)}), bf16[32,8,16,256]{3,2,1,0:T(8,128)(2,1)S(1)}, u32[]{:S(2)}, u32[]{:S(2)}) async-start(bf16[32,8,16,256]{3,2,1,0:T(8,128)(2,1)} %before.3), calls=%async_computation.1 | async-start | bytes 4194304 | tf_op jit(solution)/shard_map/all_to_all | solution.py:178
  42.6 1.3 copy-start.1
  44.0 33.7 %all-to-all-start = ((bf16[32,8,16,256]{3,2,1,0:T(8,128)(2,1)}), bf16[32,8,16,256]{3,2,1,0:T(8,128)(2,1)S(1)}, u32[]{:S(2)}, u32[]{:S(2)}) async-start(bf16[32,8,16,256]{3,2,1,0:T(8,128)(2,1)} %before.2), calls=%async_computation | async-start | bytes 4194304 | tf_op jit(solution)/shard_map/all_to_all | solution.py:178
  57.7 32.1 %copy-start.10 = (bf16[2,256,256]{2,1,0:T(8,128)(2,1)S(1)}, bf16[2,256,256]{2,1,0:T(8,128)(2,1)}, u32[]{:S(2)}) copy-start(bf16[2,256,256]{2,1,0:T(8,128)(2,1)} %get-tuple-element.30) | copy-start | bytes 786436
  57.7 33.6 %copy-start.8 = (bf16[2,256,256]{2,1,0:T(8,128)(2,1)S(1)}, bf16[2,256,256]{2,1,0:T(8,128)(2,1)}, u32[]{:S(2)}) copy-start(bf16[2,256,256]{2,1,0:T(8,128)(2,1)} %get-tuple-element.34) | copy-start | bytes 786436
  57.7 32.1 %collective-permute-start.7 = (bf16[2,256,256]{2,1,0:T(8,128)(2,1)}, bf16[2,256,256]{2,1,0:T(8,128)(2,1)S(1)}, u32[]{:S(2)}, u32[]{:S(2)}) collective-permute-start(bf16[2,256,256]{2,1,0:T(8,128)(2,1)} %get-tuple-element.29), channel_id=1, source_target_pairs={{0,194},{64,0},{128,64},{192,128},{2,192},{66,2},{130,66},{194,130... | collective-permute-start | bytes 786440 | tf_op jit(solution)/shard_map/ppermute | solution.py:130
  63.4 27.9 %collective-permute-start.11 = (bf16[2,256,256]{2,1,0:T(8,128)(2,1)}, bf16[2,256,256]{2,1,0:T(8,128)(2,1)S(1)}, u32[]{:S(2)}, u32[]{:S(2)}) collective-permute-start(bf16[2,256,256]{2,1,0:T(8,128)(2,1)} %get-tuple-element.33), channel_id=1, source_target_pairs={{0,64},{64,128},{128,192},{192,2},{2,66},{66,130},{130,194},{194,0... | collective-permute-start | bytes 786440 | tf_op jit(solution)/shard_map/ppermute | solution.py:133
  77.7 1.4 copy-start
  84.0 11.6 %copy-start.9 = (bf16[2,256,256]{2,1,0:T(8,128)(2,1)S(1)}, bf16[2,256,256]{2,1,0:T(8,128)(2,1)}, u32[]{:S(2)}) copy-start(bf16[2,256,256]{2,1,0:T(8,128)(2,1)} %get-tuple-element.26) | copy-start | bytes 786436
  84.0 15.1 %copy-start.6 = (bf16[2,256,256]{2,1,0:T(8,128)(2,1)S(1)}, bf16[2,256,256]{2,1,0:T(8,128)(2,1)}, u32[]{:S(2)}) copy-start(bf16[2,256,256]{2,1,0:T(8,128)(2,1)} %get-tuple-element.31) | copy-start | bytes 786436
  84.1 18.7 %copy-start.5 = (bf16[2,256,256]{2,1,0:T(8,128)(2,1)S(1)}, bf16[2,256,256]{2,1,0:T(8,128)(2,1)}, u32[]{:S(2)}) copy-start(bf16[2,256,256]{2,1,0:T(8,128)(2,1)} %get-tuple-element.35) | copy-start | bytes 786436
  84.1 10.4 %collective-permute-start = (bf16[2,256,256]{2,1,0:T(8,128)(2,1)}, bf16[2,256,256]{2,1,0:T(8,128)(2,1)S(1)}, u32[]{:S(2)}, u32[]{:S(2)}) collective-permute-start(bf16[2,256,256]{2,1,0:T(8,128)(2,1)} %get-tuple-element.21), channel_id=1, source_target_pairs={{0,64},{64,128},{128,192},{192,2},{2,66},{66,130},{130,194},{194,0... | collective-permute-start | bytes 786440 | tf_op jit(solution)/shard_map/ppermute | solution.py:130
  85.8 9.8 %collective-permute-start.4 = (bf16[2,256,256]{2,1,0:T(8,128)(2,1)}, bf16[2,256,256]{2,1,0:T(8,128)(2,1)S(1)}, u32[]{:S(2)}, u32[]{:S(2)}) collective-permute-start(bf16[2,256,256]{2,1,0:T(8,128)(2,1)} %get-tuple-element.25), channel_id=1, source_target_pairs={{0,194},{64,0},{128,64},{192,128},{2,192},{66,2},{130,66},{194,130... | collective-permute-start | bytes 786440 | tf_op jit(solution)/shard_map/ppermute | solution.py:133
  89.9 15.9 %copy-start.7 = (bf16[2,256,256]{2,1,0:T(8,128)(2,1)S(1)}, bf16[2,256,256]{2,1,0:T(8,128)(2,1)}, u32[]{:S(2)}) copy-start(bf16[2,256,256]{2,1,0:T(8,128)(2,1)} %get-tuple-element.23) | copy-start | bytes 786436
  89.9 9.3 %collective-permute-start.8 = (bf16[2,256,256]{2,1,0:T(8,128)(2,1)S(1)}, bf16[2,256,256]{2,1,0:T(8,128)(2,1)S(1)}, u32[]{:S(2)}, u32[]{:S(2)}) collective-permute-start(bf16[2,256,256]{2,1,0:T(8,128)(2,1)S(1)} %add_convert_fusion.5), channel_id=1, source_target_pairs={{0,194},{64,0},{128,64},{192,128},{2,192},{66,2},{130,66},{194,130... | collective-permute-start | bytes 786440 | tf_op jit(solution)/shard_map/ppermute | solution.py:130
  91.4 19.0 %copy-start.2 = (bf16[2,256,256]{2,1,0:T(8,128)(2,1)S(1)}, bf16[2,256,256]{2,1,0:T(8,128)(2,1)}, u32[]{:S(2)}) copy-start(bf16[2,256,256]{2,1,0:T(8,128)(2,1)} %get-tuple-element.32) | copy-start | bytes 786436
  91.4 11.3 %collective-permute-start.12 = (bf16[2,256,256]{2,1,0:T(8,128)(2,1)S(1)}, bf16[2,256,256]{2,1,0:T(8,128)(2,1)S(1)}, u32[]{:S(2)}, u32[]{:S(2)}) collective-permute-start(bf16[2,256,256]{2,1,0:T(8,128)(2,1)S(1)} %add_convert_fusion.2), channel_id=1, source_target_pairs={{0,64},{64,128},{128,192},{192,2},{2,66},{66,130},{130,194},{194,0... | collective-permute-start | bytes 786440 | tf_op jit(solution)/shard_map/ppermute | solution.py:133
  95.5 18.5 %copy-start.4 = (bf16[2,256,256]{2,1,0:T(8,128)(2,1)S(1)}, bf16[2,256,256]{2,1,0:T(8,128)(2,1)}, u32[]{:S(2)}) copy-start(bf16[2,256,256]{2,1,0:T(8,128)(2,1)} %get-tuple-element.27) | copy-start | bytes 786436
  95.5 10.3 %collective-permute-start.1 = (bf16[2,256,256]{2,1,0:T(8,128)(2,1)S(1)}, bf16[2,256,256]{2,1,0:T(8,128)(2,1)S(1)}, u32[]{:S(2)}, u32[]{:S(2)}) collective-permute-start(bf16[2,256,256]{2,1,0:T(8,128)(2,1)S(1)} %add_convert_fusion.11), channel_id=1, source_target_pairs={{0,64},{64,128},{128,192},{192,2},{2,66},{66,130},{130,194},{194,0... | collective-permute-start | bytes 786440 | tf_op jit(solution)/shard_map/ppermute | solution.py:130
  95.7 18.5 %copy-start.3 = (bf16[2,256,256]{2,1,0:T(8,128)(2,1)S(1)}, bf16[2,256,256]{2,1,0:T(8,128)(2,1)}, u32[]{:S(2)}) copy-start(bf16[2,256,256]{2,1,0:T(8,128)(2,1)} %get-tuple-element.24) | copy-start | bytes 786436
  95.7 18.3 %collective-permute-start.5 = (bf16[2,256,256]{2,1,0:T(8,128)(2,1)S(1)}, bf16[2,256,256]{2,1,0:T(8,128)(2,1)S(1)}, u32[]{:S(2)}, u32[]{:S(2)}) collective-permute-start(bf16[2,256,256]{2,1,0:T(8,128)(2,1)S(1)} %add_convert_fusion.8), channel_id=1, source_target_pairs={{0,194},{64,0},{128,64},{192,128},{2,192},{66,2},{130,66},{194,130... | collective-permute-start | bytes 786440 | tf_op jit(solution)/shard_map/ppermute | solution.py:133
  99.3 18.0 %copy-start.11 = (bf16[2,256,256]{2,1,0:T(8,128)(2,1)S(1)}, bf16[2,256,256]{2,1,0:T(8,128)(2,1)}, u32[]{:S(2)}) copy-start(bf16[2,256,256]{2,1,0:T(8,128)(2,1)} %get-tuple-element.36) | copy-start | bytes 786436
  99.3 11.2 %collective-permute-start.9 = (bf16[2,256,256]{2,1,0:T(8,128)(2,1)S(1)}, bf16[2,256,256]{2,1,0:T(8,128)(2,1)S(1)}, u32[]{:S(2)}, u32[]{:S(2)}) collective-permute-start(bf16[2,256,256]{2,1,0:T(8,128)(2,1)S(1)} %add_convert_fusion.4), channel_id=1, source_target_pairs={{0,194},{64,0},{128,64},{192,128},{2,192},{66,2},{130,66},{194,130... | collective-permute-start | bytes 786440 | tf_op jit(solution)/shard_map/ppermute | solution.py:130
  102.8 12.9 %collective-permute-start.13 = (bf16[2,256,256]{2,1,0:T(8,128)(2,1)S(1)}, bf16[2,256,256]{2,1,0:T(8,128)(2,1)S(1)}, u32[]{:S(2)}, u32[]{:S(2)}) collective-permute-start(bf16[2,256,256]{2,1,0:T(8,128)(2,1)S(1)} %add_convert_fusion.1), channel_id=1, source_target_pairs={{0,64},{64,128},{128,192},{192,2},{2,66},{66,130},{130,194},{194,0... | collective-permute-start | bytes 786440 | tf_op jit(solution)/shard_map/ppermute | solution.py:133
  105.8 16.7 %copy-start.12 = (bf16[2,256,256]{2,1,0:T(8,128)(2,1)S(1)}, bf16[2,256,256]{2,1,0:T(8,128)(2,1)}, u32[]{:S(2)}) copy-start(bf16[2,256,256]{2,1,0:T(8,128)(2,1)} %get-tuple-element.28) | copy-start | bytes 786436
  105.9 8.3 %collective-permute-start.2 = (bf16[2,256,256]{2,1,0:T(8,128)(2,1)S(1)}, bf16[2,256,256]{2,1,0:T(8,128)(2,1)S(1)}, u32[]{:S(2)}, u32[]{:S(2)}) collective-permute-start(bf16[2,256,256]{2,1,0:T(8,128)(2,1)S(1)} %add_convert_fusion.10), channel_id=1, source_target_pairs={{0,64},{64,128},{128,192},{192,2},{2,66},{66,130},{130,194},{194,0... | collective-permute-start | bytes 786440 | tf_op jit(solution)/shard_map/ppermute | solution.py:130
  110.5 6.8 %collective-permute-start.10 = (bf16[2,256,256]{2,1,0:T(8,128)(2,1)S(1)}, bf16[2,256,256]{2,1,0:T(8,128)(2,1)S(1)}, u32[]{:S(2)}, u32[]{:S(2)}) collective-permute-start(bf16[2,256,256]{2,1,0:T(8,128)(2,1)S(1)} %add_convert_fusion.3), channel_id=1, source_target_pairs={{0,194},{64,0},{128,64},{192,128},{2,192},{66,2},{130,66},{194,130... | collective-permute-start | bytes 786440 | tf_op jit(solution)/shard_map/ppermute | solution.py:130
  114.0 8.4 %collective-permute-start.6 = (bf16[2,256,256]{2,1,0:T(8,128)(2,1)S(1)}, bf16[2,256,256]{2,1,0:T(8,128)(2,1)S(1)}, u32[]{:S(2)}, u32[]{:S(2)}) collective-permute-start(bf16[2,256,256]{2,1,0:T(8,128)(2,1)S(1)} %add_convert_fusion.7), channel_id=1, source_target_pairs={{0,194},{64,0},{128,64},{192,128},{2,192},{66,2},{130,66},{194,130... | collective-permute-start | bytes 786440 | tf_op jit(solution)/shard_map/ppermute | solution.py:133
  114.2 8.2 %collective-permute-start.3 = (bf16[2,256,256]{2,1,0:T(8,128)(2,1)S(1)}, bf16[2,256,256]{2,1,0:T(8,128)(2,1)S(1)}, u32[]{:S(2)}, u32[]{:S(2)}) collective-permute-start(bf16[2,256,256]{2,1,0:T(8,128)(2,1)S(1)} %add_convert_fusion.9), channel_id=1, source_target_pairs={{0,64},{64,128},{128,192},{192,2},{2,66},{66,130},{130,194},{194,0... | collective-permute-start | bytes 786440 | tf_op jit(solution)/shard_map/ppermute | solution.py:130
